TPU v7x, 32 devices: a whole 2x2x4 slice. The times are simulated.
32 devices in a mesh: fsdp: 8 (over y, x, core), seq: 4 (over z).
Axes of the slice: x: 2, y: 2, z: 4, core: 2. Of those that a mesh axis runs over, the one named last changes fastest.
Arguments:
- inputs: float32 [4096, 768], P(('fsdp', 'seq')), may hold values from -6 to 6
- qkv_weight: bfloat16 [768, 2304], P(('fsdp', 'seq')), may hold values from -8 to 8
- proj_weight: bfloat16 [768, 768], P(('fsdp', 'seq')), may hold values from -2.5 to 2.5
- first_gain: bfloat16 [768], P(('fsdp', 'seq')), may hold values from 0.5 to 1.5
- first_shift: bfloat16 [768], P(('fsdp', 'seq')), may hold values from -3 to 3
- second_gain: bfloat16 [768], P(('fsdp', 'seq')), may hold values from 0.5 to 1.5
- second_shift: bfloat16 [768], P(('fsdp', 'seq')), may hold values from -3 to 3
- expert_up: bfloat16 [8, 768, 3072], P('fsdp', None, 'seq'), may hold values from -0.21875 to 0.21875
- expert_down: bfloat16 [8, 768, 3072], P('fsdp', None, 'seq'), may hold values from -0.109375 to 0.109375
- gate_logits: float32 [4096, 2], P(('fsdp', 'seq')), may hold values from -160 to 160
- routes: int32 [4096, 2], P(('fsdp', 'seq')), may hold values from 0 to 7, all different within a row; in each aligned block of 128 rows (0 to 127, 128 to 255, ...) at most 64 rows name the same one
- cotangent: float32 [4096, 768], P(('fsdp', 'seq')), may hold values from -6 to 6
Outputs:
- output: float32 [4096, 768], P(('fsdp', 'seq'))
- grad_inputs: float32 [4096, 768], P(('fsdp', 'seq'))
- grad_qkv_weight: float32 [768, 2304], P(('fsdp', 'seq'))
- grad_proj_weight: float32 [768, 768], P(('fsdp', 'seq'))
- grad_first_gain: float32 [768], P(('fsdp', 'seq'))
- grad_first_shift: float32 [768], P(('fsdp', 'seq'))
- grad_second_gain: float32 [768], P(('fsdp', 'seq'))
- grad_second_shift: float32 [768], P(('fsdp', 'seq'))
- grad_expert_up: float32 [8, 768, 3072], P('fsdp', None, 'seq')
- grad_expert_down: float32 [8, 768, 3072], P('fsdp', None, 'seq')
Inputs may be any that keep to these rules, and one draw needn't show every extreme that they name: `routes`: each row names 2 different experts. In each aligned block of 128 rows (the rows of one device) no expert is named by more than 64 rows, a bound that some block reaches.
All inputs are finite; a program needn't handle non-finite values.
Results may differ from a plain program's by a relative error of at most 0.012.
Values may be sent and summed in bfloat16 or wider, within the bound.
No kernel may reach another device: no remote copies, remote signals or barrier semaphores. Data moves between devices by JAX's collectives and lax.ppermute only.
A program may use at most 128 MiB of HBM per device.

v0:
```python
import jax
import jax.numpy as jnp
from jax import lax
from jax.sharding import PartitionSpec as P

HD = 64
epsilon = 1e-06


def layer_norm(rows_in, gain_row, shift_row):
    average = jnp.mean(rows_in, axis=-1, keepdims=True)
    centred = rows_in - average
    spread = jnp.mean(centred * centred, axis=-1, keepdims=True)
    return centred * lax.rsqrt(spread + epsilon) * gain_row + shift_row


def attention_forward(q_rows, k_rows, v_rows):
    length = q_rows.shape[0]
    block_rows = min(512, length)
    score_scale = q_rows.shape[2] ** (-0.5)
    grouped = q_rows.reshape(length // block_rows, block_rows, q_rows.shape[1], q_rows.shape[2])

    def one_block(q_block):
        scores = (
            jnp.einsum("qhd,khd->hqk", q_block, k_rows, preferred_element_type=jnp.float32)
            * score_scale
        )
        top_score = jnp.max(scores, axis=-1, keepdims=True)
        weights = jnp.exp(scores - top_score)
        totals = jnp.sum(weights, axis=-1, keepdims=True)
        probs_low = (weights / totals).astype(jnp.bfloat16)
        result = jnp.einsum(
            "hqk,khd->qhd", probs_low, v_rows, preferred_element_type=jnp.float32
        ).astype(jnp.bfloat16)
        return (result, (top_score + jnp.log(totals))[..., 0])

    results, log_totals = lax.map(one_block, grouped)
    return (results.reshape(q_rows.shape), log_totals)


def attention_backward(q_rows, k_rows, v_rows, log_totals, grad_out):
    length = q_rows.shape[0]
    block_rows = min(512, length)
    score_scale = q_rows.shape[2] ** (-0.5)
    grouped_q = q_rows.reshape(length // block_rows, block_rows, q_rows.shape[1], q_rows.shape[2])
    grouped_g = grad_out.reshape(grouped_q.shape)

    def one_block(running, pieces):
        grad_k, grad_v = running
        q_block, g_block, lse_block = pieces
        scores = (
            jnp.einsum("qhd,khd->hqk", q_block, k_rows, preferred_element_type=jnp.float32)
            * score_scale
        )
        probs_full = jnp.exp(scores - lse_block[..., None])
        probs_low = probs_full.astype(jnp.bfloat16)
        grad_v = grad_v + jnp.einsum(
            "hqk,qhd->khd", probs_low, g_block, preferred_element_type=jnp.float32
        )
        grad_p = jnp.einsum("qhd,khd->hqk", g_block, v_rows, preferred_element_type=jnp.float32)
        row_dot = jnp.sum(probs_full * grad_p, axis=-1, keepdims=True)
        grad_s = (probs_full * (grad_p - row_dot) * score_scale).astype(jnp.bfloat16)
        grad_q = jnp.einsum(
            "hqk,khd->qhd", grad_s, k_rows, preferred_element_type=jnp.float32
        ).astype(jnp.bfloat16)
        grad_k = grad_k + jnp.einsum(
            "hqk,qhd->khd", grad_s, q_block, preferred_element_type=jnp.float32
        )
        return ((grad_k, grad_v), grad_q)

    empty_grad = jnp.zeros(k_rows.shape, jnp.float32)
    (grad_k, grad_v), grad_q = lax.scan(
        one_block, (empty_grad, empty_grad), (grouped_q, grouped_g, log_totals)
    )
    return (grad_q.reshape(q_rows.shape), grad_k.astype(jnp.bfloat16), grad_v.astype(jnp.bfloat16))


def slot_table(routes, experts, capacity):
    flat_ids = routes.reshape(-1)
    labels = jnp.arange(experts, dtype=jnp.int32)
    onehot = (flat_ids[:, None] == labels[None, :]).astype(jnp.int32)
    before = jnp.cumsum(onehot, axis=0) - onehot
    return flat_ids * capacity + jnp.sum(before * onehot, axis=1)


def place_rows(entries, slot_ids, slot_count):
    return jnp.zeros((slot_count, entries.shape[1]), entries.dtype).at[slot_ids].set(entries)


def expert_forward(rows_in, up_mat, down_mat):
    pre_act = jnp.dot(rows_in, up_mat, preferred_element_type=jnp.float32)
    hidden = jax.nn.gelu(pre_act).astype(jnp.bfloat16)
    result = lax.dot_general(
        hidden, down_mat, (((1,), (1,)), ((), ())), preferred_element_type=jnp.float32
    )
    return (pre_act, hidden, result)


def expert_backward(rows_in, pre_act, hidden, grad_out, up_mat, down_mat):
    grad_hidden = jnp.dot(grad_out, down_mat, preferred_element_type=jnp.float32)
    _, gelu_back = jax.vjp(jax.nn.gelu, pre_act)
    grad_pre = gelu_back(grad_hidden)[0].astype(jnp.bfloat16)
    grad_down = lax.dot_general(
        grad_out, hidden, (((0,), (0,)), ((), ())), preferred_element_type=jnp.float32
    )
    grad_up = lax.dot_general(
        rows_in, grad_pre, (((0,), (0,)), ((), ())), preferred_element_type=jnp.float32
    )
    grad_rows = lax.dot_general(
        grad_pre, up_mat, (((1,), (1,)), ((), ())), preferred_element_type=jnp.float32
    )
    return (grad_rows, grad_up, grad_down)


def to_experts(buffer):
    return lax.all_to_all(buffer, "fsdp", split_axis=0, concat_axis=0, tiled=True)


def from_experts(buffer):
    return lax.all_to_all(buffer, "fsdp", split_axis=0, concat_axis=0, tiled=True)


def local(
    inputs,
    qkv_weight,
    proj_weight,
    first_gain,
    first_shift,
    second_gain,
    second_shift,
    expert_up,
    expert_down,
    gate_logits,
    routes,
    cotangent,
):
    tok_count, model_width = inputs.shape
    seq_count = lax.axis_size("seq")
    experts = lax.axis_size("fsdp")
    top_count = routes.shape[1]
    capacity = 4 * tok_count // experts
    slot_count = experts * capacity
    seq_len = tok_count * seq_count
    group_width = model_width // seq_count
    group_heads = group_width // HD
    qkv_full, proj_full, gain_one, shift_one, gain_two, shift_two = (
        lax.all_gather(qkv_weight, ("fsdp", "seq"), axis=0, tiled=True),
        lax.all_gather(proj_weight, ("fsdp", "seq"), axis=0, tiled=True),
        lax.all_gather(first_gain, ("fsdp", "seq"), axis=0, tiled=True),
        lax.all_gather(first_shift, ("fsdp", "seq"), axis=0, tiled=True),
        lax.all_gather(second_gain, ("fsdp", "seq"), axis=0, tiled=True),
        lax.all_gather(second_shift, ("fsdp", "seq"), axis=0, tiled=True),
    )
    gain_one = gain_one.astype(jnp.float32)
    shift_one = shift_one.astype(jnp.float32)
    gain_two = gain_two.astype(jnp.float32)
    shift_two = shift_two.astype(jnp.float32)
    attn_in = layer_norm(inputs, gain_one, shift_one).astype(jnp.bfloat16)
    qkv_rows = jnp.dot(attn_in, qkv_full, preferred_element_type=jnp.float32).astype(jnp.bfloat16)
    qkv_group = lax.all_to_all(
        qkv_rows.reshape(tok_count, 3, seq_count, group_width),
        "seq",
        split_axis=2,
        concat_axis=0,
        tiled=True,
    )
    q_rows = qkv_group[:, 0, 0].reshape(seq_len, group_heads, HD)
    k_rows = qkv_group[:, 1, 0].reshape(seq_len, group_heads, HD)
    v_rows = qkv_group[:, 2, 0].reshape(seq_len, group_heads, HD)
    heads_local, log_totals = attention_forward(q_rows, k_rows, v_rows)
    heads_out = lax.all_to_all(
        heads_local.reshape(seq_len, 1, group_width), "seq", split_axis=0, concat_axis=1, tiled=True
    ).reshape(tok_count, model_width)
    residual = inputs + jnp.dot(heads_out, proj_full, preferred_element_type=jnp.float32)
    ffn_in = layer_norm(residual, gain_two, shift_two).astype(jnp.bfloat16)
    top_logit = jnp.max(gate_logits, axis=1, keepdims=True)
    raised = jnp.exp(gate_logits - top_logit)
    gate_probs = raised / jnp.sum(raised, axis=1, keepdims=True)
    slot_ids = slot_table(routes, experts, capacity)
    sent = place_rows(jnp.repeat(ffn_in, top_count, axis=0), slot_ids, slot_count)
    arrived = to_experts(sent.reshape(experts, capacity, model_width))
    grad_entry = (
        (gate_probs[:, :, None] * cotangent[:, None, :])
        .astype(jnp.bfloat16)
        .reshape(tok_count * top_count, model_width)
    )
    grad_arrived = to_experts(
        place_rows(grad_entry, slot_ids, slot_count).reshape(experts, capacity, model_width)
    )
    up_full, down_full = (
        lax.all_gather(expert_up, "seq", axis=2, tiled=True),
        lax.all_gather(expert_down, "seq", axis=2, tiled=True),
    )
    rows_in = arrived.reshape(-1, model_width)
    pre_act, hidden, produced = expert_forward(rows_in, up_full[0], down_full[0])
    expert_out = produced.astype(jnp.bfloat16)
    grad_part, grad_up, grad_down = expert_backward(
        rows_in, pre_act, hidden, grad_arrived.reshape(-1, model_width), up_full[0], down_full[0]
    )
    grad_rows = grad_part.astype(jnp.bfloat16)
    grad_expert_up, grad_expert_down = (
        lax.psum_scatter(
            grad_up[None].astype(jnp.bfloat16), "seq", scatter_dimension=2, tiled=True
        ).astype(jnp.float32),
        lax.psum_scatter(
            grad_down[None].astype(jnp.bfloat16), "seq", scatter_dimension=2, tiled=True
        ).astype(jnp.float32),
    )
    returned = from_experts(expert_out.reshape(experts, capacity, model_width)).reshape(
        slot_count, model_width
    )
    picked = returned[slot_ids].reshape(tok_count, top_count, model_width)
    output = residual + jnp.sum(gate_probs[:, :, None] * picked.astype(jnp.float32), axis=1)
    grad_back = from_experts(grad_rows.reshape(experts, capacity, model_width)).reshape(
        slot_count, model_width
    )
    grad_ffn_in = jnp.sum(
        grad_back[slot_ids].reshape(tok_count, top_count, model_width).astype(jnp.float32), axis=1
    )
    _, second_back = jax.vjp(layer_norm, residual, gain_two, shift_two)
    grad_from_ffn, grad_gain_two, grad_shift_two = second_back(grad_ffn_in)
    grad_residual = cotangent + grad_from_ffn
    grad_mix = grad_residual.astype(jnp.bfloat16)
    grad_proj = lax.dot_general(
        heads_out, grad_mix, (((0,), (0,)), ((), ())), preferred_element_type=jnp.float32
    )
    grad_heads = lax.dot_general(
        grad_mix, proj_full, (((1,), (1,)), ((), ())), preferred_element_type=jnp.float32
    ).astype(jnp.bfloat16)
    grad_group = lax.all_to_all(
        grad_heads.reshape(tok_count, seq_count, group_width),
        "seq",
        split_axis=1,
        concat_axis=0,
        tiled=True,
    ).reshape(seq_len, group_heads, HD)
    grad_q, grad_k, grad_v = attention_backward(q_rows, k_rows, v_rows, log_totals, grad_group)
    stacked = jnp.stack([grad_q, grad_k, grad_v], axis=1).reshape(seq_len, 3, 1, group_width)
    grad_qkv = lax.all_to_all(stacked, "seq", split_axis=0, concat_axis=2, tiled=True).reshape(
        tok_count, 3 * model_width
    )
    grad_qkv_part = lax.dot_general(
        attn_in, grad_qkv, (((0,), (0,)), ((), ())), preferred_element_type=jnp.float32
    )
    grad_attn_in = lax.dot_general(
        grad_qkv, qkv_full, (((1,), (1,)), ((), ())), preferred_element_type=jnp.float32
    )
    _, first_back = jax.vjp(layer_norm, inputs, gain_one, shift_one)
    grad_from_attn, grad_gain_one, grad_shift_one = first_back(grad_attn_in)
    grad_inputs = grad_residual + grad_from_attn
    reduced = (
        lax.psum_scatter(grad_qkv_part, ("fsdp", "seq"), scatter_dimension=0, tiled=True),
        lax.psum_scatter(grad_proj, ("fsdp", "seq"), scatter_dimension=0, tiled=True),
        lax.psum_scatter(grad_gain_one, ("fsdp", "seq"), scatter_dimension=0, tiled=True),
        lax.psum_scatter(grad_shift_one, ("fsdp", "seq"), scatter_dimension=0, tiled=True),
        lax.psum_scatter(grad_gain_two, ("fsdp", "seq"), scatter_dimension=0, tiled=True),
        lax.psum_scatter(grad_shift_two, ("fsdp", "seq"), scatter_dimension=0, tiled=True),
    )
    return (
        output,
        grad_inputs,
        reduced[0],
        reduced[1],
        reduced[2],
        reduced[3],
        reduced[4],
        reduced[5],
        grad_expert_up,
        grad_expert_down,
    )


def solution(mesh):
    in_specs = (
        P(("fsdp", "seq"), None),
        P(("fsdp", "seq"), None),
        P(("fsdp", "seq"), None),
        P(("fsdp", "seq")),
        P(("fsdp", "seq")),
        P(("fsdp", "seq")),
        P(("fsdp", "seq")),
        P("fsdp", None, "seq"),
        P("fsdp", None, "seq"),
        P(("fsdp", "seq"), None),
        P(("fsdp", "seq"), None),
        P(("fsdp", "seq"), None),
    )
    out_specs = (
        P(("fsdp", "seq"), None),
        P(("fsdp", "seq"), None),
        P(("fsdp", "seq"), None),
        P(("fsdp", "seq"), None),
        P(("fsdp", "seq")),
        P(("fsdp", "seq")),
        P(("fsdp", "seq")),
        P(("fsdp", "seq")),
        P("fsdp", None, "seq"),
        P("fsdp", None, "seq"),
    )
    return jax.shard_map(local, mesh=mesh, in_specs=in_specs, out_specs=out_specs, check_vma=False)
```

profile of v0, /device:TPU:0, one launch (start us, length us, event | category | flops | bytes accessed | tf_op | source)
XLA Modules:
  0.0 763.2 jit_solution(16794710249775724188)
XLA Ops:
  13.4 42.3 %all-reduce.9 = (bf16[768]{0:T(1024)(128)(2,1)S(1)}, bf16[768]{0:T(1024)(128)(2,1)S(1)}, bf16[768]{0:T(1024)(128)(2,1)S(1)}, bf16[768]{0:T(1024)(128)(2,1)S(1)}) all-reduce(bf16[768]{0:T(1024)(128)(2,1)S(1)} %dynamic-update-slice.1, bf16[768]{0:T(1024)(128)(2,1)S(1)} %dynamic-update-slice, ...), channel_id=1, replica_groups=mesh['fsdp'=8,'seq'=4] {'fsdp','seq'}, use_global_device_ids=true, to_apply=%add.1 | all-reduce | flops 3072 | bytes 12288
  57.1 16.5 %all-gather.5.cloned.1.call-done = bf16[768,2304]{1,0:T(8,128)(2,1)} async-done(((bf16[24,2304]{1,0:T(8,128)(2,1)}), bf16[768,2304]{1,0:T(8,128)(2,1)}) %all-gather.5.cloned.1.call-update) | async-done | bytes 3538960 | tf_op jit(solution)/shard_map/all_gather | solution.py:147
  73.7 2.7 convolution_convert_fusion.2
  77.5 3.5 all-to-all-start
  85.4 12.9 %all-to-all-done = bf16[128,3,4,192]{0,3,1,2:T(8,128)(2,1)S(1)} async-done(((bf16[128,3,4,192]{0,3,1,2:T(8,128)(2,1)}), bf16[128,3,4,192]{0,3,1,2:T(8,128)(2,1)S(1)}, u32[]{:S(2)}, u32[]{:S(2)}) %all-to-all-start) | async-done | bytes 589856 | tf_op jit(solution)/shard_map/all_to_all | solution.py:160
  102.3 2.3 reduce.4
  104.6 1.8 copy.88
  106.4 2.0 reshape.275
  108.4 4.0 all-to-all-start.1
  114.3 5.6 all-to-all-done.1
  120.0 2.0 reshape.276
  121.9 1.9 copy.64
  123.8 1.7 all_to_all.63
  127.1 7.7 %all-gather.7.cloned.1.call-done = bf16[768,768]{1,0:T(8,128)(2,1)} async-done(((bf16[24,768]{1,0:T(8,128)(2,1)}), bf16[768,768]{1,0:T(8,128)(2,1)}) %all-gather.7.cloned.1.call-update) | async-done | bytes 1179664 | tf_op jit(solution)/shard_map/all_gather | solution.py:148
  134.8 1.8 fusion.78
  139.7 1.9 reshape.250
  141.6 3.1 scatter_custom_fusion
  144.6 4.2 all-to-all-start.2
  155.0 2.1 mul.249
  157.1 2.6 mul.250
  159.7 3.2 scatter_custom_fusion.1
  163.0 14.7 %all-to-all-start.4 = ((bf16[8,64,768]{2,1,0:T(8,128)(2,1)}), bf16[8,64,768]{2,1,0:T(8,128)(2,1)}, u32[]{:S(2)}, u32[]{:S(2)}) async-start(bf16[8,64,768]{2,1,0:T(8,128)(2,1)} %bitcast.103), calls=%async_computation.4 | async-start | bytes 1572864 | tf_op jit(solution)/shard_map/all_to_all | solution.py:116
  177.8 46.9 %all-gather.9.cloned.1.call-done = bf16[1,768,3072]{2,1,0:T(8,128)(2,1)} async-done(((bf16[1,768,768]{2,1,0:T(8,128)(2,1)}), bf16[1,768,3072]{2,1,0:T(8,128)(2,1)}) %all-gather.9.cloned.1.call-update) | async-done | bytes 4718608 | tf_op jit(solution)/shard_map/all_gather | solution.py:191
  224.7 8.0 %fusion.14 = f32[512,3072]{1,0:T(8,128)} fusion(bf16[512,768]{1,0:T(8,128)(2,1)} %bitcast.15, bf16[1,768,3072]{2,1,0:T(8,128)(2,1)} %all-gather.9.cloned.1.call-done), kind=kOutput, calls=%fused_computation.23 | convolution fusion | flops 2415919104 | bytes 11796480 | tf_op jit(solution)/shard_map/dot_general | solution.py:91
  232.7 81.2 %all-gather.11.cloned.1.call-done = bf16[1,768,3072]{2,1,0:T(8,128)(2,1)} async-done(((bf16[1,768,768]{2,1,0:T(8,128)(2,1)}), bf16[1,768,3072]{2,1,0:T(8,128)(2,1)}) %all-gather.11.cloned.1.call-update) | async-done | bytes 4718608 | tf_op jit(solution)/shard_map/all_gather | solution.py:192
  313.9 8.5 %fusion.7 = bf16[512,3072]{1,0:T(8,128)(2,1)S(1)} fusion(f32[512,3072]{1,0:T(8,128)} %fusion.14, bf16[512,768]{1,0:T(8,128)(2,1)} %bitcast.21, bf16[1,768,3072]{2,1,0:T(8,128)(2,1)} %all-gather.11.cloned.1.call-done), kind=kOutput, calls=%fused_computation.13 | convolution fusion | flops 2447376384 | bytes 14942208 | tf_op jit(solution)/shard_map/dot_general | solution.py:100
  324.1 5.5 fusion.16
  329.7 8.1 %fusion.17 = bf16[1,768,3072]{2,1,0:T(8,128)(2,1)} fusion(bf16[512,768]{1,0:T(8,128)(2,1)} %bitcast.21, f32[512,3072]{1,0:T(8,128)} %fusion.14), kind=kOutput, calls=%fused_computation.26 | convolution fusion | flops 2432434176 | bytes 11796480 | tf_op jit(solution)/shard_map/dot_general | solution.py:103
  337.8 8.8 %fusion.38 = bf16[512,768]{1,0:T(8,128)(2,1)} fusion(bf16[1,768,3072]{2,1,0:T(8,128)(2,1)} %all-gather.11.cloned.1.call-done, f32[512,3072]{1,0:T(8,128)} %fusion.14), kind=kOutput, calls=%fused_computation.44 | convolution fusion | flops 2430468096 | bytes 11796480 | tf_op jit(solution)/shard_map/dot_general | solution.py:93
  346.7 4.2 all-to-all-start.3
  350.9 6.8 fusion.35
  357.7 5.8 all-to-all-done.3
  363.4 4.2 all-to-all-start.5
  369.2 3.5 gather_fusion
  372.7 7.6 all-to-all-done.5
  380.3 3.5 gather_fusion.1
  383.8 2.3 reshape.229
  386.0 2.8 reduce_sum.183
  388.8 2.3 reshape.228
  391.1 2.0 multiply_reduce_fusion.3
  393.1 2.2 multiply_reduce_fusion.2
  395.9 2.0 fusion.76
  398.9 1.9 fusion.56
  400.8 2.6 convolution_convert_fusion.3
  403.4 1.7 copy.71
  405.2 4.0 all-to-all-start.6
  410.8 5.9 all-to-all-done.6
  416.7 1.8 copy.72
  418.5 1.7 squeeze.27
  420.1 2.3 fusion.42
  422.4 1.9 copy.78
  424.4 3.5 fusion.79
  427.9 5.2 fusion.45
  433.1 1.9 copy.76
  435.0 5.3 fusion.48
  441.6 3.2 pad_maximum_fusion
  444.8 56.4 %all_to_all.83 = bf16[512,3,1,192]{3,1,2,0:T(4,128)(2,1)S(1)} all-to-all(bf16[512,3,1,192]{3,1,2,0:T(4,128)(2,1)S(1)} %pad_maximum_fusion), channel_id=1, replica_groups=mesh['fsdp'=8,'seq'=4] {'seq'}, dimensions={0} | all-to-all | bytes 1179648 | tf_op jit(solution)/shard_map/all_to_all | solution.py:239
  502.8 4.1 fusion.74
  508.0 3.5 multiply_reduce_fusion.4
  511.5 39.6 %all-reduce.8 = (f32[768]{0:T(1024)S(1)}, f32[768]{0:T(1024)S(1)}, f32[768]{0:T(1024)S(1)}, f32[768]{0:T(1024)S(1)}) all-reduce(f32[768]{0:T(1024)S(1)} %get-tuple-element.48, f32[768]{0:T(1024)S(1)} %get-tuple-element.50, f32[768]{0:T(1024)S(1)} %copy-done.15, ...), channel_id=4, replica_groups=mesh['fsdp'=8,'seq'=4] {'fsdp','seq'}, use_global_device_ids=true, to_apply=%region_23.24.clone | all-reduce | flops 3072 | bytes 24576
  554.6 2.9 convert_element_type.155
  557.4 2.9 convert_element_type.158
  560.3 70.9 %reduce-scatter.7.cloned.1.call-done = f32[24,768]{1,0:T(8,128)} async-done(((f32[768,768]{1,0:T(8,128)}), f32[24,768]{1,0:T(8,128)}) %reduce-scatter.7.cloned.1.call-update) | async-done | bytes 73744 | tf_op jit(solution)/shard_map/reduce_scatter | solution.py:253
  631.2 124.8 %reduce-scatter.5.cloned.1.call-done = f32[24,2304]{1,0:T(8,128)} async-done(((f32[768,2304]{1,0:T(8,128)}), f32[24,2304]{1,0:T(8,128)}) %reduce-scatter.5.cloned.1.call-update) | async-done | bytes 221200 | tf_op jit(solution)/shard_map/reduce_scatter | solution.py:252
  (135 shorter events, 43.4 us)
Async XLA Ops:
  7.2 49.7 %copy-start = (f32[128,768]{1,0:T(8,128)S(1)}, f32[128,768]{1,0:T(8,128)}, u32[]{:S(2)}) copy-start(f32[128,768]{1,0:T(8,128)} %param.12) | copy-start | bytes 1179652
  7.2 66.5 %all-gather.5.cloned.1.call-start = ((), (), s32[]{:S(2)}) async-start(), calls=%async_computation.12 | async-start | bytes 3649536 | tf_op jit(solution)/shard_map/all_gather | solution.py:147
  7.9 126.9 %all-gather.7.cloned.1.call-start = ((), (), s32[]{:S(2)}) async-start(), calls=%async_computation.13 | async-start | bytes 1216512 | tf_op jit(solution)/shard_map/all_gather | solution.py:148
  8.7 216.0 %all-gather.9.cloned.1.call-start = ((), (), s32[]{:S(2)}) async-start(), calls=%async_computation.14 | async-start | bytes 5898240 | tf_op jit(solution)/shard_map/all_gather | solution.py:191
  9.4 304.5 %all-gather.11.cloned.1.call-start = ((), (), s32[]{:S(2)}) async-start(), calls=%async_computation.15 | async-start | bytes 5898240 | tf_op jit(solution)/shard_map/all_gather | solution.py:192
  56.9 16.8 %copy-start.13 = (f32[128]{0:T(128)}, f32[128]{0:T(128)S(1)}, u32[]{:S(2)}) copy-start(f32[128]{0:T(128)S(1)} %broadcast_multiply_fusion.2) | copy-start | bytes 1540
  57.1 16.6 %copy-start.21 = (f32[128]{0:T(128)}, f32[128]{0:T(128)S(1)}, u32[]{:S(2)}) copy-start(f32[128]{0:T(128)S(1)} %multiply_reduce_fusion.8) | copy-start | bytes 1540
  57.1 16.6 %copy-start.16 = (f32[128]{0:T(128)}, f32[128]{0:T(128)S(1)}, u32[]{:S(2)}) copy-start(f32[128]{0:T(128)S(1)} %fusion.66) | copy-start | bytes 1540
  57.1 23.9 %copy-start.20 = (s32[128,2]{0,1:T(2,128)S(1)}, s32[128,2]{0,1:T(2,128)}, u32[]{:S(2)}) copy-start(s32[128,2]{0,1:T(2,128)} %param.22) | copy-start | bytes 3076
  77.5 20.8 %all-to-all-start = ((bf16[128,3,4,192]{0,3,1,2:T(8,128)(2,1)}), bf16[128,3,4,192]{0,3,1,2:T(8,128)(2,1)S(1)}, u32[]{:S(2)}, u32[]{:S(2)}) async-start(bf16[128,3,4,192]{0,3,1,2:T(8,128)(2,1)} %copy.60), calls=%async_computation | async-start | bytes 1179648 | tf_op jit(solution)/shard_map/all_to_all | solution.py:160
  84.6 13.9 %copy-start.10 = (s32[8,2,128]{2,0,1:T(8,128)}, s32[8,2,128]{2,0,1:T(8,128)S(1)}, u32[]{:S(2)}) copy-start(s32[8,2,128]{2,0,1:T(8,128)S(1)} %reduce-window.6) | copy-start | bytes 24580
  98.5 0.7 copy-start.7
  98.5 1.3 copy-start.8
  98.5 1.9 copy-start.9
  100.3 1.5 copy-start.11
  108.4 11.6 %all-to-all-start.1 = ((bf16[4,2,12288]{2,1,0:T(2,128)(2,1)}), bf16[4,2,12288]{2,1,0:T(2,128)(2,1)}, u32[]{:S(2)}, u32[]{:S(2)}) async-start(bf16[4,2,12288]{2,1,0:T(2,128)(2,1)} %reshape.275), calls=%async_computation.1 | async-start | bytes 393216 | tf_op jit(solution)/shard_map/all_to_all | solution.py:171
  136.6 0.8 copy-start.1
  136.6 0.8 copy-start.18
  136.8 0.5 copy-start.23
  137.4 0.5 copy-start.19
  144.6 18.3 %all-to-all-start.2 = ((bf16[8,64,768]{2,1,0:T(8,128)(2,1)}), bf16[8,64,768]{2,1,0:T(8,128)(2,1)}, u32[]{:S(2)}, u32[]{:S(2)}) async-start(bf16[8,64,768]{2,1,0:T(8,128)(2,1)} %bitcast.102), calls=%async_computation.2 | async-start | bytes 1572864 | tf_op jit(solution)/shard_map/all_to_all | solution.py:116
  163.0 69.7 %all-to-all-start.4 = ((bf16[8,64,768]{2,1,0:T(8,128)(2,1)}), bf16[8,64,768]{2,1,0:T(8,128)(2,1)}, u32[]{:S(2)}, u32[]{:S(2)}) async-start(bf16[8,64,768]{2,1,0:T(8,128)(2,1)} %bitcast.103), calls=%async_computation.4 | async-start | bytes 1572864 | tf_op jit(solution)/shard_map/all_to_all | solution.py:116
  177.7 376.8 %reduce-scatter.9.cloned.1.call-start = ((), (), s32[]{:S(2)}) async-start(), calls=%async_computation.18 | async-start | bytes 5898240 | tf_op jit(solution)/shard_map/reduce_scatter | solution.py:202
  322.5 1.6 copy-start.24
  329.6 227.8 %reduce-scatter.11.cloned.1.call-start = ((), (), s32[]{:S(2)}) async-start(), calls=%async_computation.19 | async-start | bytes 5898240 | tf_op jit(solution)/shard_map/reduce_scatter | solution.py:205
  346.7 16.8 %all-to-all-start.3 = ((bf16[8,64,768]{2,1,0:T(8,128)(2,1)}), bf16[8,64,768]{2,1,0:T(8,128)(2,1)}, u32[]{:S(2)}, u32[]{:S(2)}) async-start(bf16[8,64,768]{2,1,0:T(8,128)(2,1)} %bitcast.115), calls=%async_computation.3 | async-start | bytes 1572864 | tf_op jit(solution)/shard_map/all_to_all | solution.py:120
  363.4 16.8 %all-to-all-start.5 = ((bf16[8,64,768]{2,1,0:T(8,128)(2,1)}), bf16[8,64,768]{2,1,0:T(8,128)(2,1)}, u32[]{:S(2)}, u32[]{:S(2)}) async-start(bf16[8,64,768]{2,1,0:T(8,128)(2,1)} %bitcast.114), calls=%async_computation.5 | async-start | bytes 1572864 | tf_op jit(solution)/shard_map/all_to_all | solution.py:120
  367.7 263.5 %reduce-scatter.7.cloned.1.call-start = ((), (), s32[]{:S(2)}) async-start(), calls=%async_computation.17 | async-start | bytes 2433024 | tf_op jit(solution)/shard_map/reduce_scatter | solution.py:253
  391.1 6.9 copy-start.6
  391.1 7.8 %copy-start.5 = (bf16[128,4,1,192]{0,3,1,2:T(8,128)(2,1)S(1)}, bf16[128,4,1,192]{0,3,1,2:T(8,128)(2,1)}, u32[]{:S(2)}) copy-start(bf16[128,4,1,192]{0,3,1,2:T(8,128)(2,1)} %copy.65) | copy-start | bytes 589828
  398.1 0.8 copy-start.2
  405.2 11.5 %all-to-all-start.6 = ((bf16[128,4,192]{0,2,1:T(8,128)(2,1)}), bf16[128,4,192]{0,2,1:T(8,128)(2,1)}, u32[]{:S(2)}, u32[]{:S(2)}) async-start(bf16[128,4,192]{0,2,1:T(8,128)(2,1)} %bitcast.116), calls=%async_computation.6 | async-start | bytes 393216 | tf_op jit(solution)/shard_map/all_to_all | solution.py:230
  409.2 346.8 %reduce-scatter.5.cloned.1.call-start = ((), (), s32[]{:S(2)}) async-start(), calls=%async_computation.16 | async-start | bytes 7299072 | tf_op jit(solution)/shard_map/reduce_scatter | solution.py:252
  420.1 7.7 %copy-start.12 = (f32[3,512]{1,0:T(4,128)S(1)}, f32[3,512]{1,0:T(4,128)}, u32[]{:S(2)}) copy-start(f32[3,512]{1,0:T(4,128)} %log_add_fusion) | copy-start | bytes 18436
  441.6 61.2 %copy-start.14 = (f32[128]{0:T(128)S(1)}, f32[128]{0:T(128)}, u32[]{:S(2)}) copy-start(f32[128]{0:T(128)} %copy-done.13) | copy-start | bytes 1540
  441.6 61.2 %copy-start.17 = (f32[128]{0:T(128)S(1)}, f32[128]{0:T(128)}, u32[]{:S(2)}) copy-start(f32[128]{0:T(128)} %copy-done.16) | copy-start | bytes 1540
  506.9 1.0 copy-start.4
  506.9 4.6 copy-start.15
  506.9 46.5 %copy-start.22 = (f32[128]{0:T(128)S(1)}, f32[128]{0:T(128)}, u32[]{:S(2)}) copy-start(f32[128]{0:T(128)} %copy-done.21) | copy-start | bytes 1540
  508.0 45.7 %copy-start.3 = (f32[128,768]{1,0:T(8,128)S(1)}, f32[128,768]{1,0:T(8,128)}, u32[]{:S(2)}) copy-start(f32[128,768]{1,0:T(8,128)} %copy-done.2) | copy-start | bytes 1179652
Sparse Core Ops, SparseCore 0:
  10.8 62.8 all-gather.4
  76.5 58.2 all-gather.6
  136.4 88.2 all-gather.8
  226.1 87.7 all-gather.10
  329.8 84.7 reduce-scatter.8
  416.7 104.2 reduce-scatter.10
  526.8 104.2 reduce-scatter.6
  637.4 118.5 reduce-scatter.4
where the time goes:
time: 774 us; the launch traced here: 763 us
  waiting for transfers between devices  388 us (50%)
  blocking collectives  138 us (18%)
  matrix products  80.9 us (10%)
  local copies, waits for them, and re-layouts  63 us (8%)
  starting transfers between devices  39.6 us (5%)
  other arithmetic  37.9 us (5%)
  between operations  15.1 us (2%)
    reduce_scatter x1, waiting for transfers between devices, local(): lax.psum_scatter(grad_qkv_part, ('fsdp', 'seq'), scatter_dimension=0, til...  125 us
    unnamed x2, blocking collectives  81.9 us
    all_gather x1, waiting for transfers between devices, local(): lax.all_gather(expert_down, 'seq', axis=2, tiled=True)  81.2 us
    reduce_scatter x1, waiting for transfers between devices, local(): lax.psum_scatter(grad_proj, ('fsdp', 'seq'), scatter_dimension=0, tiled=T...  70.9 us
    all_to_all x1, blocking collectives, local(): lax.all_to_all(stacked, 'seq', split_axis=0, concat_axis=2, tiled=True)  56.4 us
    all_gather x1, waiting for transfers between devices, local(): lax.all_gather(expert_up, 'seq', axis=2, tiled=True)  46.9 us
    all_to_all x2, starting transfers between devices, to_experts(): lax.all_to_all(buffer, 'fsdp', split_axis=0, concat_axis=0, tiled=True)  18.9 us
    unnamed x66, local copies, waits for them, and re-layouts  16.6 us
  transfers between devices with their start and end apart: 15, of which 11 were waited for; matrix products, arithmetic and copies ran while one was open for 21% of the time, Pallas kernels for 0%

commit v1 on v0

--- a/solution.py
+++ b/solution.py
@@ -5,6 +5,27 @@
 
 HD = 64
 epsilon = 1e-06
+
+
+def ring_gather(value, axis, dim):
+    size, index, rows = (lax.axis_size(axis), lax.axis_index(axis), value.shape[dim])
+    right = [(i, (i + 1) % size) for i in range(size)]
+    behind = [(i, (i - 1) % size) for i in range(size)]
+    result = jnp.zeros((*value.shape[:dim], size * rows, *value.shape[dim + 1 :]), value.dtype)
+    result = lax.dynamic_update_slice_in_dim(result, value, index * rows, axis=dim)
+    from_left = from_right = value
+    half = size // 2
+    for step in range(1, half + 1):
+        from_left = lax.ppermute(from_left, axis, right)
+        result = lax.dynamic_update_slice_in_dim(
+            result, from_left, (index - step) % size * rows, axis=dim
+        )
+        if step < size - half:
+            from_right = lax.ppermute(from_right, axis, behind)
+            result = lax.dynamic_update_slice_in_dim(
+                result, from_right, (index + step) % size * rows, axis=dim
+            )
+    return result
 
 
 def layer_norm(rows_in, gain_row, shift_row):
@@ -189,7 +210,7 @@
     )
     up_full, down_full = (
         lax.all_gather(expert_up, "seq", axis=2, tiled=True),
-        lax.all_gather(expert_down, "seq", axis=2, tiled=True),
+        ring_gather(expert_down, "seq", 2),
     )
     rows_in = arrived.reshape(-1, model_width)
     pre_act, hidden, produced = expert_forward(rows_in, up_full[0], down_full[0])

time: 774 us -> 726 us (0.938)
  waiting for transfers between devices: 388 us -> 306 us
  blocking collectives: 138 us -> 171 us
  local copies, waits for them, and re-layouts: 63 us -> 71.6 us
    all_gather x1 -> x0, waiting for transfers between devices: 81.2 us -> none  [local(): lax.all_gather(expert_down, 'seq', axis=2, tiled=True)]
    unnamed x2, blocking collectives: 81.9 us -> 114 us
    all_gather x1, waiting for transfers between devices: 7.73 us -> 25 us  [local(): lax.all_gather(proj_weight, ('fsdp', 'seq'), axis=0, tiled=True)]
    all_gather x1, waiting for transfers between devices: 16.5 us -> 0.02 us  [local(): lax.all_gather(qkv_weight, ('fsdp', 'seq'), axis=0, tiled=True)]
    all_to_all x2, starting transfers between devices: 18.9 us -> 8.89 us  [to_experts(): lax.all_to_all(buffer, 'fsdp', split_axis=0, concat_axis=0, tiled=True)]
    dynamic_update_slice x0 -> x4, local copies, waits for them, and re-layouts: none -> 8.52 us  [the longest x2 4.94 us: ring_gather(): lax.dynamic_update_slice_in_dim(result, from_left, (index - step) % size...]
    unnamed x66 -> x70, local copies, waits for them, and re-layouts: 16.6 us -> 15.7 us
  transfers between devices with their start and end apart: 15 -> 17, of which waited for: 11 -> 8; matrix products, arithmetic and copies ran while one was open for 21% -> 23% of each run, Pallas kernels for 0% -> 0%
where the time goes in v1:
time: 726 us; the launch traced here: 717 us
  waiting for transfers between devices  306 us (42%)
  blocking collectives  171 us (24%)
  matrix products  80.2 us (11%)
  local copies, waits for them, and re-layouts  71.6 us (10%)
  starting transfers between devices  37.5 us (5%)
  other arithmetic  35.2 us (5%)
  between operations  15.1 us (2%)
    reduce_scatter x1, waiting for transfers between devices, local(): lax.psum_scatter(grad_qkv_part, ('fsdp', 'seq'), scatter_dimension=0, til...  125 us
    unnamed x2, blocking collectives  114 us
    reduce_scatter x1, waiting for transfers between devices, local(): lax.psum_scatter(grad_proj, ('fsdp', 'seq'), scatter_dimension=0, tiled=T...  70.7 us
    all_to_all x1, blocking collectives, local(): lax.all_to_all(stacked, 'seq', split_axis=0, concat_axis=2, tiled=True)  56.5 us
    all_gather x1, waiting for transfers between devices, local(): lax.all_gather(expert_up, 'seq', axis=2, tiled=True)  50.1 us
    all_gather x1, waiting for transfers between devices, local(): lax.all_gather(proj_weight, ('fsdp', 'seq'), axis=0, tiled=True)  25 us
    unnamed x70, local copies, waits for them, and re-layouts  15.7 us
  transfers between devices with their start and end apart: 17, of which 8 were waited for; matrix products, arithmetic and copies ran while one was open for 23% of the time, Pallas kernels for 0%

profile of v1, /device:TPU:0, one launch (start us, length us, event | category | flops | bytes accessed | tf_op | source)
XLA Modules:
  0.0 716.9 jit_solution(8244464965263804085)
XLA Ops:
  9.4 5.1 collective-permute-start.1
  19.0 74.9 %all-reduce.9 = (bf16[768]{0:T(1024)(128)(2,1)S(1)}, bf16[768]{0:T(1024)(128)(2,1)S(1)}, bf16[768]{0:T(1024)(128)(2,1)S(1)}, bf16[768]{0:T(1024)(128)(2,1)S(1)}) all-reduce(bf16[768]{0:T(1024)(128)(2,1)S(1)} %dynamic-update-slice.1, bf16[768]{0:T(1024)(128)(2,1)S(1)} %dynamic-update-slice, ...), channel_id=1, replica_groups=mesh['fsdp'=8,'seq'=4] {'fsdp','seq'}, use_global_device_ids=true, to_apply=%add.1 | all-reduce | flops 3072 | bytes 12288
  96.2 2.8 convolution_convert_fusion.2
  100.2 4.2 all-to-all-start
  106.2 14.5 %all-to-all-done = bf16[128,3,4,192]{0,3,1,2:T(8,128)(2,1)S(1)} async-done(((bf16[128,3,4,192]{0,3,1,2:T(8,128)(2,1)}), bf16[128,3,4,192]{0,3,1,2:T(8,128)(2,1)S(1)}, u32[]{:S(2)}, u32[]{:S(2)}) %all-to-all-start) | async-done | bytes 589856 | tf_op jit(solution)/shard_map/all_to_all | solution.py:181
  127.4 4.0 all-to-all-start.1
  133.2 2.7 squeeze.34
  137.0 2.0 collective-permute-start.2
  139.0 2.0 reshape.284
  141.0 1.9 copy.64
  146.1 25.0 %all-gather.6.cloned.1.call-done = bf16[768,768]{1,0:T(8,128)(2,1)} async-done(((bf16[24,768]{1,0:T(8,128)(2,1)}), bf16[768,768]{1,0:T(8,128)(2,1)}) %all-gather.6.cloned.1.call-update) | async-done | bytes 1179664 | tf_op jit(solution)/shard_map/all_gather | solution.py:169
  171.2 1.8 fusion.69
  176.1 1.9 reshape.258
  178.0 3.1 scatter_custom_fusion
  181.1 4.7 all-to-all-start.2
  190.0 2.1 mul.265
  192.2 2.6 mul.266
  194.8 3.2 scatter_custom_fusion.1
  198.0 2.5 bitcast_dynamic-update-slice_fusion.2
  200.5 2.4 bitcast_dynamic-update-slice_fusion.1
  203.0 4.2 all-to-all-start.4
  207.3 2.4 bitcast_dynamic-update-slice_fusion
  209.7 50.1 %all-gather.8.cloned.1.call-done = bf16[1,768,3072]{2,1,0:T(8,128)(2,1)} async-done(((bf16[1,768,768]{2,1,0:T(8,128)(2,1)}), bf16[1,768,3072]{2,1,0:T(8,128)(2,1)}) %all-gather.8.cloned.1.call-update) | async-done | bytes 4718608 | tf_op jit(solution)/shard_map/all_gather | solution.py:212
  259.8 7.9 %fusion.10 = f32[512,3072]{1,0:T(8,128)} fusion(bf16[512,768]{1,0:T(8,128)(2,1)} %bitcast.15, bf16[1,768,3072]{2,1,0:T(8,128)(2,1)} %all-gather.8.cloned.1.call-done), kind=kOutput, calls=%fused_computation.19 | convolution fusion | flops 2415919104 | bytes 11796480 | tf_op jit(solution)/shard_map/dot_general | solution.py:112
  267.6 8.5 %fusion.7 = bf16[512,3072]{1,0:T(8,128)(2,1)S(1)} fusion(f32[512,3072]{1,0:T(8,128)} %fusion.10, bf16[512,768]{1,0:T(8,128)(2,1)} %bitcast.24, bf16[768,3072]{1,0:T(8,128)(2,1)} %bitcast_dynamic-update-slice_fusion), kind=kOutput, calls=%fused_computation.13 | convolution fusion | flops 2447376384 | bytes 14942208 | tf_op jit(solution)/shard_map/dot_general | solution.py:121
  276.2 1.7 copy-done.26
  277.9 5.5 fusion.12
  283.7 8.1 %fusion.13 = bf16[1,768,3072]{2,1,0:T(8,128)(2,1)} fusion(bf16[512,768]{1,0:T(8,128)(2,1)} %bitcast.24, f32[512,3072]{1,0:T(8,128)} %fusion.10), kind=kOutput, calls=%fused_computation.22 | convolution fusion | flops 2432434176 | bytes 11796480 | tf_op jit(solution)/shard_map/dot_general | solution.py:124
  291.8 8.8 %convolution_convert_fusion.3 = bf16[512,768]{1,0:T(8,128)(2,1)} fusion(bf16[768,3072]{1,0:T(8,128)(2,1)} %bitcast_dynamic-update-slice_fusion, f32[512,3072]{1,0:T(8,128)} %fusion.10), kind=kOutput, calls=%fused_computation.40 | convolution fusion | flops 2430468096 | bytes 11796480 | tf_op jit(solution)/shard_map/dot_general | solution.py:114
  300.7 4.2 all-to-all-start.3
  304.9 6.8 fusion.29
  311.7 5.8 all-to-all-done.3
  317.5 4.2 all-to-all-start.5
  323.2 3.5 gather_fusion
  326.7 7.6 %all-to-all-done.5 = bf16[8,64,768]{2,1,0:T(8,128)(2,1)} async-done(((bf16[8,64,768]{2,1,0:T(8,128)(2,1)}), bf16[8,64,768]{2,1,0:T(8,128)(2,1)}, u32[]{:S(2)}, u32[]{:S(2)}) %all-to-all-start.5) | async-done | bytes 786464 | tf_op jit(solution)/shard_map/all_to_all | solution.py:141
  334.3 3.5 gather_fusion.1
  337.8 2.3 reshape.237
  340.0 2.8 reduce_sum.183
  342.8 2.3 reshape.236
  345.1 2.0 multiply_reduce_fusion.3
  347.1 2.2 multiply_reduce_fusion.2
  350.0 2.0 fusion.67
  352.9 1.9 fusion.47
  354.8 2.6 convolution_convert_fusion.4
  357.4 1.7 copy.71
  359.2 4.0 all-to-all-start.6
  364.8 5.8 all-to-all-done.6
  370.5 1.8 copy.72
  372.3 1.7 squeeze.39
  374.0 2.3 fusion.33
  376.3 1.9 copy.78
  378.2 3.5 fusion.70
  381.7 5.2 fusion.36
  387.0 1.9 copy.76
  388.9 5.3 fusion.39
  395.5 3.2 pad_maximum_fusion
  398.7 56.5 %all_to_all.83 = bf16[512,3,1,192]{3,1,2,0:T(4,128)(2,1)S(1)} all-to-all(bf16[512,3,1,192]{3,1,2,0:T(4,128)(2,1)S(1)} %pad_maximum_fusion), channel_id=1, replica_groups=mesh['fsdp'=8,'seq'=4] {'seq'}, dimensions={0} | all-to-all | bytes 1179648 | tf_op jit(solution)/shard_map/all_to_all | solution.py:260
  456.6 4.1 fusion.65
  461.9 3.5 multiply_reduce_fusion.4
  465.4 39.5 %all-reduce.8 = (f32[768]{0:T(1024)S(1)}, f32[768]{0:T(1024)S(1)}, f32[768]{0:T(1024)S(1)}, f32[768]{0:T(1024)S(1)}) all-reduce(f32[768]{0:T(1024)S(1)} %get-tuple-element.48, f32[768]{0:T(1024)S(1)} %get-tuple-element.50, f32[768]{0:T(1024)S(1)} %copy-done.15, ...), channel_id=4, replica_groups=mesh['fsdp'=8,'seq'=4] {'fsdp','seq'}, use_global_device_ids=true, to_apply=%region_23.24.clone | all-reduce | flops 3072 | bytes 24576
  508.3 2.9 convert_element_type.155
  511.1 2.9 convert_element_type.158
  514.0 70.7 %reduce-scatter.7.cloned.1.call-done = f32[24,768]{1,0:T(8,128)} async-done(((f32[768,768]{1,0:T(8,128)}), f32[24,768]{1,0:T(8,128)}) %reduce-scatter.7.cloned.1.call-update) | async-done | bytes 73744 | tf_op jit(solution)/shard_map/reduce_scatter | solution.py:274
  584.7 124.9 %reduce-scatter.5.cloned.1.call-done = f32[24,2304]{1,0:T(8,128)} async-done(((f32[768,2304]{1,0:T(8,128)}), f32[24,2304]{1,0:T(8,128)}) %reduce-scatter.5.cloned.1.call-update) | async-done | bytes 221200 | tf_op jit(solution)/shard_map/reduce_scatter | solution.py:273
  (147 shorter events, 44.2 us)
Async XLA Ops:
  7.2 89.0 %all-gather.4.cloned.1.call-start = ((), (), s32[]{:S(2)}) async-start(), calls=%async_computation.12 | async-start | bytes 3649536 | tf_op jit(solution)/shard_map/all_gather | solution.py:168
  7.9 163.2 %all-gather.6.cloned.1.call-start = ((), (), s32[]{:S(2)}) async-start(), calls=%async_computation.13 | async-start | bytes 1216512 | tf_op jit(solution)/shard_map/all_gather | solution.py:169
  8.7 251.1 %all-gather.8.cloned.1.call-start = ((), (), s32[]{:S(2)}) async-start(), calls=%async_computation.14 | async-start | bytes 5898240 | tf_op jit(solution)/shard_map/all_gather | solution.py:212
  9.4 191.1 %collective-permute-start.1 = (bf16[1,768,768]{2,1,0:T(8,128)(2,1)}, bf16[1,768,768]{2,1,0:T(8,128)(2,1)}, u32[]{:S(2)}, u32[]{:S(2)}) collective-permute-start(bf16[1,768,768]{2,1,0:T(8,128)(2,1)} %param.20), channel_id=1, source_target_pairs={{0,3},{1,0},{2,1},{3,2},{4,7},{5,4},{6,5},{7,6},{8,11},{9,8},{10,9... | collective-permute-start | bytes 3538952 | tf_op jit(solution)/shard_map/ppermute | solution.py:24
  14.5 122.5 %collective-permute-start = (bf16[1,768,768]{2,1,0:T(8,128)(2,1)}, bf16[1,768,768]{2,1,0:T(8,128)(2,1)}, u32[]{:S(2)}, u32[]{:S(2)}) collective-permute-start(bf16[1,768,768]{2,1,0:T(8,128)(2,1)} %param.20), channel_id=1, source_target_pairs={{0,1},{1,2},{2,3},{3,0},{4,5},{5,6},{6,7},{7,4},{8,9},{9,10},{10,1... | collective-permute-start | bytes 3538952 | tf_op jit(solution)/shard_map/ppermute | solution.py:19
  95.0 5.3 copy-start.13
  96.1 4.1 copy-start.23
  96.2 4.1 copy-start.16
  96.2 8.2 %copy-start.22 = (s32[128,2]{0,1:T(2,128)S(1)}, s32[128,2]{0,1:T(2,128)}, u32[]{:S(2)}) copy-start(s32[128,2]{0,1:T(2,128)} %param.22) | copy-start | bytes 3076
  96.2 9.3 %copy-start.18 = (f32[128,2]{0,1:T(2,128)S(1)}, f32[128,2]{0,1:T(2,128)}, u32[]{:S(2)}) copy-start(f32[128,2]{0,1:T(2,128)} %param.21) | copy-start | bytes 3076
  100.2 20.5 %all-to-all-start = ((bf16[128,3,4,192]{0,3,1,2:T(8,128)(2,1)}), bf16[128,3,4,192]{0,3,1,2:T(8,128)(2,1)S(1)}, u32[]{:S(2)}, u32[]{:S(2)}) async-start(bf16[128,3,4,192]{0,3,1,2:T(8,128)(2,1)} %copy.60), calls=%async_computation | async-start | bytes 1179648 | tf_op jit(solution)/shard_map/all_to_all | solution.py:181
  105.5 25.9 %copy-start.20 = (f32[128]{0:T(128)}, f32[128]{0:T(128)S(1)}, u32[]{:S(2)}) copy-start(f32[128]{0:T(128)S(1)} %reduce_max.20) | copy-start | bytes 1540
  120.8 0.7 copy-start.8
  120.8 1.3 copy-start.9
  120.8 1.9 copy-start.10
  122.7 0.8 copy-start.11
  127.4 11.6 %all-to-all-start.1 = ((bf16[4,2,12288]{2,1,0:T(2,128)(2,1)}), bf16[4,2,12288]{2,1,0:T(2,128)(2,1)}, u32[]{:S(2)}, u32[]{:S(2)}) async-start(bf16[4,2,12288]{2,1,0:T(2,128)(2,1)} %reshape.283), calls=%async_computation.1 | async-start | bytes 393216 | tf_op jit(solution)/shard_map/all_to_all | solution.py:192
  133.2 2.7 copy-start.7
  135.9 35.3 %copy-start = (f32[128,768]{1,0:T(8,128)S(1)}, f32[128,768]{1,0:T(8,128)}, u32[]{:S(2)}) copy-start(f32[128,768]{1,0:T(8,128)} %param.12) | copy-start | bytes 1179652
  137.0 70.2 %collective-permute-start.2 = (bf16[1,768,768]{2,1,0:T(8,128)(2,1)}, bf16[1,768,768]{2,1,0:T(8,128)(2,1)}, u32[]{:S(2)}, u32[]{:S(2)}) collective-permute-start(bf16[1,768,768]{2,1,0:T(8,128)(2,1)} %collective-permute-done), channel_id=1, source_target_pairs={{0,1},{1,2},{2,3},{3,0},{4,5},{5,6},{6,7},{7,4},{8,9},{9,10},{10,1... | collective-permute-start | bytes 3538952 | tf_op jit(solution)/shard_map/ppermute | solution.py:19
  173.0 0.8 copy-start.1
  173.0 0.8 copy-start.19
  173.2 0.6 copy-start.25
  173.8 0.5 copy-start.21
  181.1 21.9 %all-to-all-start.2 = ((bf16[8,64,768]{2,1,0:T(8,128)(2,1)}), bf16[8,64,768]{2,1,0:T(8,128)(2,1)}, u32[]{:S(2)}, u32[]{:S(2)}) async-start(bf16[8,64,768]{2,1,0:T(8,128)(2,1)} %bitcast.103), calls=%async_computation.2 | async-start | bytes 1572864 | tf_op jit(solution)/shard_map/all_to_all | solution.py:137
  203.0 64.7 %all-to-all-start.4 = ((bf16[8,64,768]{2,1,0:T(8,128)(2,1)}), bf16[8,64,768]{2,1,0:T(8,128)(2,1)}, u32[]{:S(2)}, u32[]{:S(2)}) async-start(bf16[8,64,768]{2,1,0:T(8,128)(2,1)} %bitcast.104), calls=%async_computation.4 | async-start | bytes 1572864 | tf_op jit(solution)/shard_map/all_to_all | solution.py:137
  207.2 301.1 %reduce-scatter.9.cloned.1.call-start = ((), (), s32[]{:S(2)}) async-start(), calls=%async_computation.17 | async-start | bytes 5898240 | tf_op jit(solution)/shard_map/reduce_scatter | solution.py:223
  276.2 1.7 copy-start.26
  283.5 227.7 %reduce-scatter.11.cloned.1.call-start = ((), (), s32[]{:S(2)}) async-start(), calls=%async_computation.18 | async-start | bytes 5898240 | tf_op jit(solution)/shard_map/reduce_scatter | solution.py:226
  300.7 16.8 %all-to-all-start.3 = ((bf16[8,64,768]{2,1,0:T(8,128)(2,1)}), bf16[8,64,768]{2,1,0:T(8,128)(2,1)}, u32[]{:S(2)}, u32[]{:S(2)}) async-start(bf16[8,64,768]{2,1,0:T(8,128)(2,1)} %bitcast.116), calls=%async_computation.3 | async-start | bytes 1572864 | tf_op jit(solution)/shard_map/all_to_all | solution.py:141
  317.5 16.8 %all-to-all-start.5 = ((bf16[8,64,768]{2,1,0:T(8,128)(2,1)}), bf16[8,64,768]{2,1,0:T(8,128)(2,1)}, u32[]{:S(2)}, u32[]{:S(2)}) async-start(bf16[8,64,768]{2,1,0:T(8,128)(2,1)} %bitcast.115), calls=%async_computation.5 | async-start | bytes 1572864 | tf_op jit(solution)/shard_map/all_to_all | solution.py:141
  321.7 263.0 %reduce-scatter.7.cloned.1.call-start = ((), (), s32[]{:S(2)}) async-start(), calls=%async_computation.16 | async-start | bytes 2433024 | tf_op jit(solution)/shard_map/reduce_scatter | solution.py:274
  345.1 6.9 copy-start.6
  345.1 7.8 %copy-start.5 = (bf16[128,4,1,192]{0,3,1,2:T(8,128)(2,1)S(1)}, bf16[128,4,1,192]{0,3,1,2:T(8,128)(2,1)}, u32[]{:S(2)}) copy-start(bf16[128,4,1,192]{0,3,1,2:T(8,128)(2,1)} %copy.65) | copy-start | bytes 589828
  352.1 0.7 copy-start.2
  359.2 11.4 %all-to-all-start.6 = ((bf16[128,4,192]{0,2,1:T(8,128)(2,1)}), bf16[128,4,192]{0,2,1:T(8,128)(2,1)}, u32[]{:S(2)}, u32[]{:S(2)}) async-start(bf16[128,4,192]{0,2,1:T(8,128)(2,1)} %bitcast.117), calls=%async_computation.6 | async-start | bytes 393216 | tf_op jit(solution)/shard_map/all_to_all | solution.py:251
  363.2 346.4 %reduce-scatter.5.cloned.1.call-start = ((), (), s32[]{:S(2)}) async-start(), calls=%async_computation.15 | async-start | bytes 7299072 | tf_op jit(solution)/shard_map/reduce_scatter | solution.py:273
  374.0 7.7 %copy-start.12 = (f32[3,512]{1,0:T(4,128)S(1)}, f32[3,512]{1,0:T(4,128)}, u32[]{:S(2)}) copy-start(f32[3,512]{1,0:T(4,128)} %log_add_fusion) | copy-start | bytes 18436
  395.4 61.2 %copy-start.14 = (f32[128]{0:T(128)S(1)}, f32[128]{0:T(128)}, u32[]{:S(2)}) copy-start(f32[128]{0:T(128)} %copy-done.13) | copy-start | bytes 1540
  395.5 61.2 %copy-start.17 = (f32[128]{0:T(128)S(1)}, f32[128]{0:T(128)}, u32[]{:S(2)}) copy-start(f32[128]{0:T(128)} %copy-done.16) | copy-start | bytes 1540
  460.8 1.0 copy-start.4
  460.8 4.6 copy-start.15
  460.8 46.4 %copy-start.24 = (f32[128]{0:T(128)S(1)}, f32[128]{0:T(128)}, u32[]{:S(2)}) copy-start(f32[128]{0:T(128)} %copy-done.23) | copy-start | bytes 1540
  461.8 45.6 %copy-start.3 = (f32[128,768]{1,0:T(8,128)S(1)}, f32[128,768]{1,0:T(8,128)}, u32[]{:S(2)}) copy-start(f32[128,768]{1,0:T(8,128)} %copy-done.2) | copy-start | bytes 1179652
Sparse Core Ops, SparseCore 0:
  10.8 84.1 all-gather.3
  97.8 73.3 all-gather.5
  172.7 86.9 all-gather.7
  283.6 84.6 reduce-scatter.8
  370.5 104.1 reduce-scatter.10
  480.4 104.2 reduce-scatter.6
  590.9 118.5 reduce-scatter.4
